TPU v7x, 128 devices: a whole 4x4x4 slice. The times are simulated.
128 devices in a mesh: wide: 16 (over y_hi, z, core), narrow: 8 (over x, y_lo).
Axes of the slice: x: 4, y: 4 (y_hi: 2, y_lo: 2; y = y_hi * 2 + y_lo), z: 4, core: 2. Of those that a mesh axis runs over, the one named last changes fastest.
Arguments:
- density: float32 [128, 2, 512, 512], P(('wide', 'narrow')), may hold values from -6 to 6
- hamiltonian: bfloat16 [2, 512, 512], replicated, may hold values from -0.1875 to 0.1875
- left_operators: bfloat16 [7, 2, 512, 512], replicated, may hold values from -0.25 to 0.25
- right_operators: bfloat16 [7, 2, 512, 512], replicated, may hold values from -0.25 to 0.25
- block_mask: int32 [7, 2, 8, 8], replicated, may hold values 0 or 1
- operator_slot: int32 [7], replicated, may hold values from 0 to 6, each once
- flip_sign: int32 [7], replicated, may hold values from 0 to 1
- damping_rate: float32 [7], replicated, may hold values from 0.2 to 2
- lower_weight: float32 [7], replicated, may hold values from 0.5 to 2
Outputs:
- derivative: float32 [128, 2, 512, 512], P(('wide', 'narrow'))
Inputs may be any that keep to these rules, and one draw needn't show every extreme that they name: `operator_slot`: each of the 7 slots is used by exactly one mode.
All inputs are finite; a program needn't handle non-finite values.
Results may differ from a plain program's by a relative error of at most 0.0023.
Values may be sent and summed in bfloat16 or wider, within the bound.
A program may use at most 128 MiB of HBM per device.

v0:
```python
import functools

import jax
import jax.numpy as jnp
from jax import lax
from jax.experimental import pallas as pl
from jax.experimental.pallas import tpu as pltpu
from jax.sharding import PartitionSpec as P

MESH = pl.DeviceIdType.MESH
F32, BF16 = jnp.float32, jnp.bfloat16
N, BS, MODES, NB = 512, 64, 7, 8
CH = 128
NC = N // CH
SUB = 32
NS = N // SUB
PER = CH // SUB
OWN = MODES
RINGS = (
    (0, 6, (0, 1), (8, 1)),
    (1, 2, (0, 2), (0, 6)),
    (4, 5, (2, 0), (6, 0)),
)
CORE = 3


def kernel(
    slot_ref, flip_ref, rate_ref, lower_ref, mask_ref, dens_hbm, ham_hbm, left_hbm, right_hbm, out_hbm,
    rho, left, right, ham, acc, rows_ref, coef, out_sem, dens_sem, ham_sem, left_sem, right_sem, send_sem, recv_sem,
):
    wide, narrow = lax.axis_index("wide"), lax.axis_index("narrow")
    index = wide * 8 + narrow

    def peer(masks):
        return (wide ^ masks[0], narrow ^ masks[1])

    dens = [
        pltpu.make_async_copy(
            dens_hbm.at[0, :, pl.ds(c * CH, CH), :], acc.at[:, pl.ds(c * CH, CH), :], dens_sem.at[c])
        for c in range(NC)
    ]
    for copy in dens:
        copy.start()
    ham_copy = pltpu.make_async_copy(ham_hbm, ham, ham_sem)
    ham_copy.start()
    loads = []
    for s in range(MODES):
        loads.append((
            pltpu.make_async_copy(left_hbm.at[s], left.at[s], left_sem.at[s]),
            pltpu.make_async_copy(right_hbm.at[s], right.at[s], right_sem.at[s]),
        ))
    for pair in loads:
        for copy in pair:
            copy.start()

    barrier = pltpu.get_barrier_semaphore()
    peers = [(1, 0)] + [m for r in RINGS for m in r[2:]]
    for masks in peers:
        pl.semaphore_signal(barrier, inc=1, device_id=peer(masks), device_id_type=MESH)

    rate = jnp.float32(0.0)
    below = jnp.int32(0)
    for k in range(MODES):
        bit = (index // 2**k) % 2
        parity = (1 - 2 * (below % 2)).astype(F32)
        sign = (1 - 2 * flip_ref[k]).astype(F32)
        on = bit.astype(F32)
        coef[k] = parity * sign * (on * lower_ref[k] + (1.0 - on))
        rate = rate + on * rate_ref[k]
        below = below + bit
    coef[OWN] = jnp.float32(1.0)

    spread = (
        lax.broadcasted_iota(jnp.int32, (NB, N), 1) // BS == lax.broadcasted_iota(jnp.int32, (NB, N), 0)
    ).astype(F32)
    for s in range(MODES):
        for side in range(2):
            rows_ref[s, side] = jnp.dot(mask_ref[s, side].astype(F32), spread, preferred_element_type=F32)

    def send(k, s, masks, src):
        at = (s // PER, slice(None), pl.ds(pl.multiple_of((s % PER) * SUB, SUB), SUB), slice(None))
        return pltpu.make_async_remote_copy(
            src_ref=rho.at[(src,) + at], dst_ref=rho.at[(k,) + at],
            send_sem=send_sem.at[k, s], recv_sem=recv_sem.at[k, s],
            device_id=peer(masks), device_id_type=MESH)

    def send_own(s):
        for low, _, near, _ in RINGS:
            send(low, s, near, OWN).start()
        send(CORE, s, (1, 0), OWN).start()

    def forward(s):
        for low, high, near, far in RINGS:
            send(low, s, near, OWN).wait_recv()
            send(high, s, far, low).start()

    for c in range(NC):
        dens[c].wait()
        rows = pl.ds(c * CH, CH)
        value = acc[:, rows, :]
        rho[OWN, c] = value.astype(BF16)
        acc[:, rows, :] = (-rate) * value
        if c == 0:
            pl.semaphore_wait(barrier, len(peers))
        else:
            for s in range((c - 1) * PER, c * PER):
                send_own(s)
    ham_copy.wait()
    left[OWN, 0] = ham[1]
    left[OWN, 1] = -ham[0]
    right[OWN, 0] = -ham[1]
    right[OWN, 1] = ham[0]
    for s in range((NC - 1) * PER, NS):
        send_own(s)

    def step(k, slot, c):
        rows = pl.ds(pl.multiple_of(c * CH, CH), CH)
        weight = coef[k]
        real, imag = rho[k, c, 0], rho[k, c, 1]
        both = jnp.concatenate([real, imag], axis=0)
        lr, li = left[slot, 0, :, rows], left[slot, 1, :, rows]
        acc[0] += weight * jnp.dot(jnp.concatenate([lr, -li], axis=1), both, preferred_element_type=F32)
        acc[1] += weight * jnp.dot(jnp.concatenate([li, lr], axis=1), both, preferred_element_type=F32)
        wide_rows = jnp.concatenate([
            jnp.concatenate([real, -imag], axis=1), jnp.concatenate([imag, real], axis=1)], axis=0)
        ops = jnp.concatenate([right[slot, 0], right[slot, 1]], axis=0)
        value = jnp.dot(wide_rows, ops, preferred_element_type=F32)
        acc[0, rows, :] += weight * value[:CH]
        acc[1, rows, :] += weight * value[CH:]

    @pl.loop(0, NC)
    def _(c):
        step(OWN, OWN, c)

    forward(0)
    for s in range(MODES):
        for copy in loads[s]:
            copy.wait()

        @pl.loop(0, NB)
        def _(i):
            rows = pl.ds(pl.multiple_of(i * BS, BS), BS)
            for side, ops in ((0, left), (1, right)):
                keep = rows_ref[s, side, pl.ds(i, 1), :].astype(BF16)
                ops[s, 0, rows, :] = ops[s, 0, rows, :] * keep
                ops[s, 1, rows, :] = ops[s, 1, rows, :] * keep

        if s % 3 == 2:
            forward(1 + s // 3)

    @pl.loop(0, NC)
    def _(c):
        for s in range(PER):
            send(CORE, c * PER + s, (1, 0), OWN).wait_recv()
        step(CORE, slot_ref[CORE], c)

        @pl.when(c % 2 == 1)
        def _():
            forward(3 + c // 2)

    done = 5
    for c in range(NC):
        for r, (low, high, near, far) in enumerate(RINGS):
            while done < (c + 1) * PER or done < min(NS, (c + 1) * PER + r):
                forward(done)
                done += 1
            step(low, slot_ref[low], c)
        for low, high, near, far in RINGS:
            if done < min(NS, (c + 2) * PER) :
                forward(done)
                done += 1
            for s in range(c * PER, (c + 1) * PER):
                send(high, s, far, low).wait_recv()
            step(high, slot_ref[high], c)

    out = pltpu.make_async_copy(acc, out_hbm.at[0], out_sem)
    out.start()
    for s in range(NS):
        for low, high, near, far in RINGS:
            send(low, s, near, OWN).wait_send()
            send(high, s, far, low).wait_send()
        send(CORE, s, (1, 0), OWN).wait_send()
    out.wait()


def body(density, hamiltonian, left_operators, right_operators, block_mask, operator_slot, flip_sign, damping_rate, lower_weight):
    smem, vmem, anywhere = (pl.BlockSpec(memory_space=m) for m in (pltpu.SMEM, pltpu.VMEM, pl.ANY))
    return pl.pallas_call(
        kernel,
        out_shape=jax.ShapeDtypeStruct((1, 2, N, N), F32),
        in_specs=[smem] * 4 + [vmem] + [anywhere] * 4,
        out_specs=anywhere,
        scratch_shapes=[
            pltpu.VMEM((MODES + 1, NC, 2, CH, N), BF16),
            pltpu.VMEM((MODES + 1, 2, N, N), BF16),
            pltpu.VMEM((MODES + 1, 2, N, N), BF16),
            pltpu.VMEM((2, N, N), BF16),
            pltpu.VMEM((2, N, N), F32),
            pltpu.VMEM((MODES, 2, NB, N), F32),
            pltpu.SMEM((MODES + 1,), F32),
            pltpu.SemaphoreType.DMA,
            pltpu.SemaphoreType.DMA((NC,)),
            pltpu.SemaphoreType.DMA,
            pltpu.SemaphoreType.DMA((MODES,)),
            pltpu.SemaphoreType.DMA((MODES,)),
            pltpu.SemaphoreType.DMA((MODES, NS)),
            pltpu.SemaphoreType.DMA((MODES, NS)),
        ],
        compiler_params=pltpu.CompilerParams(
            collective_id=0, has_side_effects=True, vmem_limit_bytes=60 * 1024 * 1024),
        name="heom",
    )(operator_slot, flip_sign, damping_rate, lower_weight, block_mask, density, hamiltonian, left_operators, right_operators)


def solution(mesh):
    placed = (P(("wide", "narrow"), None, None, None), P(), P(), P(), P(), P(), P(), P(), P())
    return jax.shard_map(
        body, mesh=mesh, in_specs=placed, out_specs=P(("wide", "narrow"), None, None, None), check_vma=False)
```

profile of v0, /device:TPU:0, one launch (start us, length us, event | category | flops | bytes accessed | tf_op | source)
XLA Modules:
  0.0 45.2 jit_solution(5954394816991149431)
XLA Ops:
  0.0 42.1 %heom.1 = f32[1,2,512,512]{3,2,1,0:T(8,128)} custom-call(s32[7]{0:T(128)} %slot_ref.1, s32[7]{0:T(128)} %flip_ref.1, f32[7]{0:T(128)} %rate_ref.1, f32[7]{0:T(128)} %lower_ref.1, s32[7,2,8,8]{3,2,1,0:T(8,128)} %mask_ref.1, f32[1,2,512,512]{3,2,1,0:T(8,128)} %dens_hbm.1, bf16[2,512,512]{2,1,0:T(8,128)(2,1)} %ham_hbm.1, bf16[7,2,512,512]{3,2,1,0:T(8,128)(2,1)} %left_hbm.1, ...), custom_call_target="tpu_custom_call" | custom-call | tf_op jit(solution)/shard_map/heom/pallas_call | solution.py:188
  42.1 3.1 %copy.11 = f32[1,2,512,512]{3,2,1,0:T(8,128)} copy(f32[1,2,512,512]{3,2,1,0:T(8,128)} %heom.1) | data formatting | bytes 4194304
where the time goes:
time: 45.4 us; the launch traced here: 45.2 us
  Pallas kernels  42.1 us (93%)
  local copies, waits for them, and re-layouts  3.08 us (7%)
    pallas_call x1, Pallas kernels, body(): pl.pallas_call(kernel, out_shape=jax.ShapeDtypeStruct((1, 2, N, N), F32),...  42.1 us
    unnamed x1, local copies, waits for them, and re-layouts  3.08 us

commit v1 on v0

v1 whole, which is shorter than its diff:
```python
import jax
import jax.numpy as jnp
from jax import lax
from jax.experimental import pallas as pl
from jax.experimental.pallas import tpu as pltpu
from jax.sharding import PartitionSpec as P

MESH = pl.DeviceIdType.MESH
F32, BF16 = jnp.float32, jnp.bfloat16
N, BS, MODES, NB = 512, 64, 7, 8
CH = 128
NC = N // CH
SUB = 64
NS = N // SUB
PER = CH // SUB
MODE_AT = (0, 1, 4, 6, 2, 5, 3)
CORE, OWN = 6, 7
NEAR = ((0, 1), (0, 2), (2, 0))
FAR = ((8, 1), (0, 6), (6, 0))
OTHER = (1, 0)
RINGS = range(3)


def plan():
    def forward(s):
        return [("forward", None, s)]

    def steps(places, c):
        return [("step", p, c) for p in places]

    near, far = (0, 1, 2), (3, 4, 5)
    out = [("step", OWN, c) for c in range(NC)] + forward(0)
    out += [("mask", None, s) for s in range(MODES)]
    out += steps([CORE], 0) + forward(1) + steps([CORE], 1) + steps([CORE], 2) + steps([CORE], 3) + forward(2)
    out += steps(near, 0) + forward(3)
    out += steps(near, 1) + steps(far[:1], 0) + forward(4)
    out += steps(far[1:], 0) + forward(5)
    out += steps(near, 2) + forward(6)
    out += steps(far, 1) + forward(7)
    out += steps(near, 3) + steps(far, 2) + steps(far, 3)
    return out


PLAN = plan()


def kernel(
    slot_hbm, flip_hbm, rate_hbm, lower_hbm, mask_hbm, dens_hbm, ham_hbm, left_hbm, right_hbm, out_ref,
    rho, left, right, ham, rows_ref, coef, slot_at, slot_ref, flip_ref, rate_ref, lower_ref, mask_ref,
    small_sem, dens_sem, ham_sem, left_sem, right_sem, send_sem, recv_sem,
):
    wide, narrow = lax.axis_index("wide"), lax.axis_index("narrow")
    index = wide * 8 + narrow
    acc = out_ref.at[0]

    def peer(masks):
        return (wide ^ masks[0], narrow ^ masks[1])

    barrier = pltpu.get_barrier_semaphore()
    peers = (OTHER,) + NEAR + FAR
    for masks in peers:
        pl.semaphore_signal(barrier, inc=1, device_id=peer(masks), device_id_type=MESH)

    dens = [
        pltpu.make_async_copy(
            dens_hbm.at[0, :, pl.ds(s * SUB, SUB), :], acc.at[:, pl.ds(s * SUB, SUB), :], dens_sem.at[s])
        for s in range(NS)
    ]
    for copy in dens:
        copy.start()
    small = [
        pltpu.make_async_copy(src, dst, small_sem.at[i])
        for i, (src, dst) in enumerate((
            (rate_hbm, rate_ref), (flip_hbm, flip_ref), (lower_hbm, lower_ref), (slot_hbm, slot_ref), (mask_hbm, mask_ref)))
    ]
    for copy in small:
        copy.start()
    ham_copy = pltpu.make_async_copy(ham_hbm, ham, ham_sem)
    ham_copy.start()

    def load(s):
        return (
            pltpu.make_async_copy(left_hbm.at[s], left.at[s], left_sem.at[s]),
            pltpu.make_async_copy(right_hbm.at[s], right.at[s], right_sem.at[s]),
        )

    for copy in small[:4]:
        copy.wait()
    rate = jnp.float32(0.0)
    below = jnp.int32(0)
    for k in range(MODES):
        place = MODE_AT.index(k)
        bit = (index // 2**k) % 2
        parity = (1 - 2 * (below % 2)).astype(F32)
        sign = (1 - 2 * flip_ref[k]).astype(F32)
        on = bit.astype(F32)
        coef[place] = parity * sign * (on * lower_ref[k] + (1.0 - on))
        slot_at[place] = slot_ref[k]
        rate = rate + on * rate_ref[k]
        below = below + bit
    coef[OWN] = jnp.float32(1.0)

    def send(place, s, masks, src):
        return pltpu.make_async_remote_copy(
            src_ref=rho.at[src, s], dst_ref=rho.at[place, s],
            send_sem=send_sem.at[place, s], recv_sem=recv_sem.at[place, s],
            device_id=peer(masks), device_id_type=MESH)

    def send_own(s):
        for r in RINGS:
            send(r, s, NEAR[r], OWN).start()
        send(CORE, s, OTHER, OWN).start()

    def forward(s):
        for r in RINGS:
            send(r, s, NEAR[r], OWN).wait_recv()
            send(3 + r, s, FAR[r], r).start()

    for s in range(NS):
        dens[s].wait()
        rows = pl.ds(s * SUB, SUB)
        value = acc[:, rows, :]
        rho[OWN, s] = value.astype(BF16)
        acc[:, rows, :] = (-rate) * value
        if s == 0:
            pl.semaphore_wait(barrier, len(peers))
        else:
            send_own(s - 1)
        if s == NS // 2:
            for i in range(MODES):
                for copy in load(i):
                    copy.start()
    ham_copy.wait()
    left[OWN, 0] = ham[1]
    left[OWN, 1] = -ham[0]
    right[OWN, 0] = -ham[1]
    right[OWN, 1] = ham[0]
    send_own(NS - 1)

    small[4].wait()
    spread = (
        lax.broadcasted_iota(jnp.int32, (NB, N), 1) // BS == lax.broadcasted_iota(jnp.int32, (NB, N), 0)
    ).astype(F32)

    rows_ref[...] = jnp.dot(
        mask_ref[...].reshape(MODES * 2 * NB, NB).astype(F32), spread, preferred_element_type=F32
    ).reshape(MODES, 2, NB, N)

    def left_part(place, c):
        slot, weight = OWN if place == OWN else slot_at[place], coef[place]
        rows = pl.ds(c * CH, CH)
        both = jnp.concatenate([rho[place, c * PER + s, i] for i in range(2) for s in range(PER)], axis=0)
        lr, li = left[slot, 0, :, rows], left[slot, 1, :, rows]
        acc[0] += weight * jnp.dot(jnp.concatenate([lr, -li], axis=1), both, preferred_element_type=F32)
        acc[1] += weight * jnp.dot(jnp.concatenate([li, lr], axis=1), both, preferred_element_type=F32)

    def right_part(place, first, count):
        slot, weight = OWN if place == OWN else slot_at[place], coef[place]
        rows = pl.ds(first * SUB, count * SUB)
        real, imag = (jnp.concatenate([rho[place, first + s, i] for s in range(count)], axis=0) for i in range(2))
        wide_rows = jnp.concatenate([
            jnp.concatenate([real, -imag], axis=1), jnp.concatenate([imag, real], axis=1)], axis=0)
        ops = jnp.concatenate([right[slot, 0], right[slot, 1]], axis=0)
        value = jnp.dot(wide_rows, ops, preferred_element_type=F32)
        acc[0, rows, :] += weight * value[: count * SUB]
        acc[1, rows, :] += weight * value[count * SUB :]

    def step(place, c):
        left_part(place, c)
        right_part(place, c * PER, PER)

    def mask(s):
        for copy in load(s):
            copy.wait()
        for i in range(NB):
            rows = pl.ds(i * BS, BS)
            for side, ops in ((0, left), (1, right)):
                keep = rows_ref[s, side, i : i + 1, :].astype(BF16)
                ops[s, 0, rows, :] = ops[s, 0, rows, :] * keep
                ops[s, 1, rows, :] = ops[s, 1, rows, :] * keep

    def arrived(place, s):
        if place == CORE:
            send(CORE, s, OTHER, OWN).wait_recv()
        elif place >= 3 and place != OWN:
            send(place, s, FAR[place - 3], place - 3).wait_recv()

    for what, place, c in PLAN:
        if what == "forward":
            forward(c)
        elif what == "mask":
            mask(c)
        elif what == "step":
            for s in range(c * PER, (c + 1) * PER):
                arrived(place, s)
            step(place, c)
        elif what == "right":
            arrived(place, c)
            right_part(place, c, 1)
        else:
            left_part(place, c)

    @pl.loop(0, NS)
    def _(s):
        for r in RINGS:
            send(r, s, NEAR[r], OWN).wait_send()
            send(3 + r, s, FAR[r], r).wait_send()
        send(CORE, s, OTHER, OWN).wait_send()


def body(density, hamiltonian, left_operators, right_operators, block_mask, operator_slot, flip_sign, damping_rate, lower_weight):
    vmem, anywhere = (pl.BlockSpec(memory_space=m) for m in (pltpu.VMEM, pl.ANY))
    return pl.pallas_call(
        kernel,
        out_shape=pltpu.VMEM((1, 2, N, N), F32),
        in_specs=[anywhere] * 9,
        out_specs=vmem,
        scratch_shapes=[
            pltpu.VMEM((MODES + 1, NS, 2, SUB, N), BF16),
            pltpu.VMEM((MODES + 1, 2, N, N), BF16),
            pltpu.VMEM((MODES + 1, 2, N, N), BF16),
            pltpu.VMEM((2, N, N), BF16),
            pltpu.VMEM((MODES, 2, NB, N), F32),
            pltpu.SMEM((MODES + 1,), F32),
            pltpu.SMEM((MODES + 1,), jnp.int32),
            pltpu.SMEM((MODES,), jnp.int32),
            pltpu.SMEM((MODES,), jnp.int32),
            pltpu.SMEM((MODES,), F32),
            pltpu.SMEM((MODES,), F32),
            pltpu.VMEM((MODES, 2, NB, NB), jnp.int32),
            pltpu.SemaphoreType.DMA((5,)),
            pltpu.SemaphoreType.DMA((NS,)),
            pltpu.SemaphoreType.DMA,
            pltpu.SemaphoreType.DMA((MODES,)),
            pltpu.SemaphoreType.DMA((MODES,)),
            pltpu.SemaphoreType.DMA((MODES, NS)),
            pltpu.SemaphoreType.DMA((MODES, NS)),
        ],
        compiler_params=pltpu.CompilerParams(
            collective_id=0, has_side_effects=True, vmem_limit_bytes=58 * 1024 * 1024),
        name="heom",
    )(operator_slot, flip_sign, damping_rate, lower_weight, block_mask, density, hamiltonian, left_operators, right_operators)


def solution(mesh):
    placed = (P(("wide", "narrow"), None, None, None), P(), P(), P(), P(), P(), P(), P(), P())
    return jax.shard_map(
        body, mesh=mesh, in_specs=placed, out_specs=P(("wide", "narrow"), None, None, None), check_vma=False)
```

time: 45.4 us -> 40.1 us (0.88)
  Pallas kernels: 42.1 us -> 38.6 us
  local copies, waits for them, and re-layouts: 3.08 us -> 1.32 us
    pallas_call x1, Pallas kernels: 42.1 us -> 38.6 us  [body(): pl.pallas_call(kernel, out_shape=pltpu.VMEM((1, 2, N, N), F32), in_specs=...]
    unnamed x1, local copies, waits for them, and re-layouts: 3.08 us -> 1.32 us
where the time goes in v1:
time: 40.1 us; the launch traced here: 40 us
  Pallas kernels  38.6 us (96%)
  local copies, waits for them, and re-layouts  1.32 us (3%)
    pallas_call x1, Pallas kernels, body(): pl.pallas_call(kernel, out_shape=pltpu.VMEM((1, 2, N, N), F32), in_specs=...  38.6 us
    unnamed x1, local copies, waits for them, and re-layouts  1.32 us

profile of v1, /device:TPU:0, one launch (start us, length us, event | category | flops | bytes accessed | tf_op | source)
XLA Modules:
  0.0 40.0 jit_solution(7018533619218464228)
XLA Ops:
  0.0 38.6 %heom.1 = f32[1,2,512,512]{3,2,1,0:T(8,128)S(1)} custom-call(s32[7]{0:T(128)} %slot_hbm.1, s32[7]{0:T(128)} %flip_hbm.1, f32[7]{0:T(128)} %rate_hbm.1, f32[7]{0:T(128)} %lower_hbm.1, s32[7,2,8,8]{3,2,1,0:T(8,128)} %mask_hbm.1, f32[1,2,512,512]{3,2,1,0:T(8,128)} %dens_hbm.1, bf16[2,512,512]{2,1,0:T(8,128)(2,1)} %ham_hbm.1, bf16[7,2,512,512]{3,2,1,0:T(8,128)(2,1)} %left_hbm.1, ...), custom_call_target="tpu_custom_call" | custom-call | tf_op jit(solution)/shard_map/heom/pallas_call | solution.py:213
  38.6 1.3 %copy.11 = f32[1,2,512,512]{3,2,1,0:T(8,128)} copy(f32[1,2,512,512]{3,2,1,0:T(8,128)S(1)} %heom.1) | data formatting | bytes 4194304

commit v2 on v1

--- a/solution.py
+++ b/solution.py
@@ -18,6 +18,8 @@
 NEAR = ((0, 1), (0, 2), (2, 0))
 FAR = ((8, 1), (0, 6), (6, 0))
 OTHER = (1, 0)
+LAST = NS - 1
+ORDER = (0, LAST) + tuple(range(1, LAST))
 RINGS = range(3)
 
 
@@ -28,16 +30,20 @@
     def steps(places, c):
         return [("step", p, c) for p in places]
 
+    def group(places, c):
+        return [("group", places, c)]
+
     near, far = (0, 1, 2), (3, 4, 5)
     out = [("step", OWN, c) for c in range(NC)] + forward(0)
     out += [("mask", None, s) for s in range(MODES)]
-    out += steps([CORE], 0) + forward(1) + steps([CORE], 1) + steps([CORE], 2) + steps([CORE], 3) + forward(2)
-    out += steps(near, 0) + forward(3)
-    out += steps(near, 1) + steps(far[:1], 0) + forward(4)
-    out += steps(far[1:], 0) + forward(5)
-    out += steps(near, 2) + forward(6)
-    out += steps(far, 1) + forward(7)
-    out += steps(near, 3) + steps(far, 2) + steps(far, 3)
+    out += steps([CORE], 0) + forward(1) + [("relay", None, LAST)]
+    out += steps([CORE], 1) + steps([CORE], 2) + steps([CORE], 3) + forward(2)
+    out += group(near, 0) + forward(3)
+    out += group(near, 1) + steps(far[:1], 0) + forward(4)
+    out += group(far[1:], 0) + forward(5)
+    out += group(near, 2) + steps(far[:1], 1) + forward(6)
+    out += group(far[1:], 1) + forward(7)
+    out += group(near, 3) + group(far, 2) + group(far, 3)
     return out
 
 
@@ -46,8 +52,8 @@
 
 def kernel(
     slot_hbm, flip_hbm, rate_hbm, lower_hbm, mask_hbm, dens_hbm, ham_hbm, left_hbm, right_hbm, out_ref,
-    rho, left, right, ham, rows_ref, coef, slot_at, slot_ref, flip_ref, rate_ref, lower_ref, mask_ref,
-    small_sem, dens_sem, ham_sem, left_sem, right_sem, send_sem, recv_sem,
+    rho, relay, left, right, ham, rows_ref, coef, slot_at, slot_ref, flip_ref, rate_ref, lower_ref, mask_ref,
+    small_sem, dens_sem, ham_sem, left_sem, right_sem, send_sem, recv_sem, relay_send, relay_recv,
 ):
     wide, narrow = lax.axis_index("wide"), lax.axis_index("narrow")
     index = wide * 8 + narrow
@@ -66,8 +72,8 @@
             dens_hbm.at[0, :, pl.ds(s * SUB, SUB), :], acc.at[:, pl.ds(s * SUB, SUB), :], dens_sem.at[s])
         for s in range(NS)
     ]
-    for copy in dens:
-        copy.start()
+    for s in ORDER:
+        dens[s].start()
     small = [
         pltpu.make_async_copy(src, dst, small_sem.at[i])
         for i, (src, dst) in enumerate((
@@ -106,36 +112,56 @@
             send_sem=send_sem.at[place, s], recv_sem=recv_sem.at[place, s],
             device_id=peer(masks), device_id_type=MESH)
 
-    def send_own(s):
+    def pass_by(r):
+        return pltpu.make_async_remote_copy(
+            src_ref=rho.at[OWN, LAST], dst_ref=relay.at[r], send_sem=relay_send.at[r], recv_sem=relay_recv.at[r],
+            device_id=peer(FAR[r]), device_id_type=MESH)
+
+    def pass_on(r):
+        return pltpu.make_async_remote_copy(
+            src_ref=relay.at[r], dst_ref=rho.at[3 + r, LAST],
+            send_sem=send_sem.at[3 + r, LAST], recv_sem=recv_sem.at[3 + r, LAST],
+            device_id=peer(NEAR[r]), device_id_type=MESH)
+
+    def send_near(s):
         for r in RINGS:
             send(r, s, NEAR[r], OWN).start()
         send(CORE, s, OTHER, OWN).start()
 
+    def send_own(s):
+        if s == LAST:
+            for r in RINGS:
+                pass_by(r).start()
+        else:
+            send_near(s)
+
     def forward(s):
         for r in RINGS:
             send(r, s, NEAR[r], OWN).wait_recv()
-            send(3 + r, s, FAR[r], r).start()
-
-    for s in range(NS):
+            if s != LAST:
+                send(3 + r, s, FAR[r], r).start()
+
+    for i, s in enumerate(ORDER):
         dens[s].wait()
         rows = pl.ds(s * SUB, SUB)
         value = acc[:, rows, :]
         rho[OWN, s] = value.astype(BF16)
         acc[:, rows, :] = (-rate) * value
-        if s == 0:
+        if i == 0:
             pl.semaphore_wait(barrier, len(peers))
         else:
-            send_own(s - 1)
-        if s == NS // 2:
-            for i in range(MODES):
-                for copy in load(i):
+            send_own(ORDER[i - 1])
+        if i == NS // 2:
+            for j in range(MODES):
+                for copy in load(j):
                     copy.start()
     ham_copy.wait()
     left[OWN, 0] = ham[1]
     left[OWN, 1] = -ham[0]
     right[OWN, 0] = -ham[1]
     right[OWN, 1] = ham[0]
-    send_own(NS - 1)
+    send_own(ORDER[-1])
+    send_near(LAST)
 
     small[4].wait()
     spread = (
@@ -153,6 +179,18 @@
         lr, li = left[slot, 0, :, rows], left[slot, 1, :, rows]
         acc[0] += weight * jnp.dot(jnp.concatenate([lr, -li], axis=1), both, preferred_element_type=F32)
         acc[1] += weight * jnp.dot(jnp.concatenate([li, lr], axis=1), both, preferred_element_type=F32)
+
+    def left_group(places, c):
+        rows = pl.ds(c * CH, CH)
+        real, imag = 0.0, 0.0
+        for place in places:
+            slot, weight = slot_at[place], coef[place]
+            both = jnp.concatenate([rho[place, c * PER + s, i] for i in range(2) for s in range(PER)], axis=0)
+            lr, li = left[slot, 0, :, rows], left[slot, 1, :, rows]
+            real += weight * jnp.dot(jnp.concatenate([lr, -li], axis=1), both, preferred_element_type=F32)
+            imag += weight * jnp.dot(jnp.concatenate([li, lr], axis=1), both, preferred_element_type=F32)
+        acc[0] += real
+        acc[1] += imag
 
     def right_part(place, first, count):
         slot, weight = OWN if place == OWN else slot_at[place], coef[place]
@@ -188,17 +226,26 @@
     for what, place, c in PLAN:
         if what == "forward":
             forward(c)
+        elif what == "relay":
+            for r in RINGS:
+                pass_by(r).wait_recv()
+                pass_on(r).start()
         elif what == "mask":
             mask(c)
         elif what == "step":
             for s in range(c * PER, (c + 1) * PER):
                 arrived(place, s)
             step(place, c)
-        elif what == "right":
-            arrived(place, c)
-            right_part(place, c, 1)
         else:
-            left_part(place, c)
+            for p in place:
+                for s in range(c * PER, (c + 1) * PER):
+                    arrived(p, s)
+            left_group(place, c)
+            for p in place:
+                right_part(p, c * PER, PER)
+
+    for r in RINGS:
+        pass_by(r).wait_send()
 
     @pl.loop(0, NS)
     def _(s):
@@ -217,6 +264,7 @@
         out_specs=vmem,
         scratch_shapes=[
             pltpu.VMEM((MODES + 1, NS, 2, SUB, N), BF16),
+            pltpu.VMEM((3, 2, SUB, N), BF16),
             pltpu.VMEM((MODES + 1, 2, N, N), BF16),
             pltpu.VMEM((MODES + 1, 2, N, N), BF16),
             pltpu.VMEM((2, N, N), BF16),
@@ -235,6 +283,8 @@
             pltpu.SemaphoreType.DMA((MODES,)),
             pltpu.SemaphoreType.DMA((MODES, NS)),
             pltpu.SemaphoreType.DMA((MODES, NS)),
+            pltpu.SemaphoreType.DMA((3,)),
+            pltpu.SemaphoreType.DMA((3,)),
         ],
         compiler_params=pltpu.CompilerParams(
             collective_id=0, has_side_effects=True, vmem_limit_bytes=58 * 1024 * 1024),

time: 40.1 us -> 38.1 us (0.950)
  Pallas kernels: 38.6 us -> 36.6 us
    pallas_call x1, Pallas kernels: 38.6 us -> 36.6 us  [body(): pl.pallas_call(kernel, out_shape=pltpu.VMEM((1, 2, N, N), F32), in_specs=...]
where the time goes in v2:
time: 38.1 us; the launch traced here: 38 us
  Pallas kernels  36.6 us (96%)
  local copies, waits for them, and re-layouts  1.32 us (3%)
    pallas_call x1, Pallas kernels, body(): pl.pallas_call(kernel, out_shape=pltpu.VMEM((1, 2, N, N), F32), in_specs=...  36.6 us
    unnamed x1, local copies, waits for them, and re-layouts  1.32 us

profile of v2, /device:TPU:0, one launch (start us, length us, event | category | flops | bytes accessed | tf_op | source)
XLA Modules:
  0.0 38.0 jit_solution(3788252792594222501)
XLA Ops:
  0.0 36.6 %heom.1 = f32[1,2,512,512]{3,2,1,0:T(8,128)S(1)} custom-call(s32[7]{0:T(128)} %slot_hbm.1, s32[7]{0:T(128)} %flip_hbm.1, f32[7]{0:T(128)} %rate_hbm.1, f32[7]{0:T(128)} %lower_hbm.1, s32[7,2,8,8]{3,2,1,0:T(8,128)} %mask_hbm.1, f32[1,2,512,512]{3,2,1,0:T(8,128)} %dens_hbm.1, bf16[2,512,512]{2,1,0:T(8,128)(2,1)} %ham_hbm.1, bf16[7,2,512,512]{3,2,1,0:T(8,128)(2,1)} %left_hbm.1, ...), custom_call_target="tpu_custom_call" | custom-call | tf_op jit(solution)/shard_map/heom/pallas_call | solution.py:260
  36.6 1.3 %copy.11 = f32[1,2,512,512]{3,2,1,0:T(8,128)} copy(f32[1,2,512,512]{3,2,1,0:T(8,128)S(1)} %heom.1) | data formatting | bytes 4194304

commit v3 on v2

--- a/solution.py
+++ b/solution.py
@@ -19,6 +19,7 @@
 FAR = ((8, 1), (0, 6), (6, 0))
 OTHER = (1, 0)
 LAST = NS - 1
+LATE = NS - 2
 ORDER = (0, LAST) + tuple(range(1, LAST))
 RINGS = range(3)
 
@@ -36,13 +37,13 @@
     near, far = (0, 1, 2), (3, 4, 5)
     out = [("step", OWN, c) for c in range(NC)] + forward(0)
     out += [("mask", None, s) for s in range(MODES)]
-    out += steps([CORE], 0) + forward(1) + [("relay", None, LAST)]
+    out += steps([CORE], 0) + forward(1) + [("relay", 0, LAST)]
     out += steps([CORE], 1) + steps([CORE], 2) + steps([CORE], 3) + forward(2)
     out += group(near, 0) + forward(3)
     out += group(near, 1) + steps(far[:1], 0) + forward(4)
     out += group(far[1:], 0) + forward(5)
     out += group(near, 2) + steps(far[:1], 1) + forward(6)
-    out += group(far[1:], 1) + forward(7)
+    out += group(far[1:], 1) + [("late", 1, LATE)] + forward(7) + [("relay", 1, LAST)]
     out += group(near, 3) + group(far, 2) + group(far, 3)
     return out
 
@@ -57,6 +58,7 @@
 ):
     wide, narrow = lax.axis_index("wide"), lax.axis_index("narrow")
     index = wide * 8 + narrow
+    core = wide % 2
     acc = out_ref.at[0]
 
     def peer(masks):
@@ -138,7 +140,11 @@
     def forward(s):
         for r in RINGS:
             send(r, s, NEAR[r], OWN).wait_recv()
-            if s != LAST:
+            if s == LATE:
+                @pl.when(core == 0)
+                def _():
+                    send(3 + r, s, FAR[r], r).start()
+            elif s != LAST:
                 send(3 + r, s, FAR[r], r).start()
 
     for i, s in enumerate(ORDER):
@@ -226,10 +232,17 @@
     for what, place, c in PLAN:
         if what == "forward":
             forward(c)
+        elif what == "late":
+            @pl.when(core == 1)
+            def _():
+                for r in RINGS:
+                    send(3 + r, c, FAR[r], r).start()
         elif what == "relay":
-            for r in RINGS:
-                pass_by(r).wait_recv()
-                pass_on(r).start()
+            @pl.when(core == place)
+            def _():
+                for r in RINGS:
+                    pass_by(r).wait_recv()
+                    pass_on(r).start()
         elif what == "mask":
             mask(c)
         elif what == "step":

time: 38.1 us -> 37.5 us (0.984)
  Pallas kernels: 36.6 us -> 36 us
    pallas_call x1, Pallas kernels: 36.6 us -> 36 us  [body(): pl.pallas_call(kernel, out_shape=pltpu.VMEM((1, 2, N, N), F32), in_specs=...]
where the time goes in v3:
time: 37.5 us; the launch traced here: 37.4 us
  Pallas kernels  36 us (96%)
  local copies, waits for them, and re-layouts  1.32 us (4%)
    pallas_call x1, Pallas kernels, body(): pl.pallas_call(kernel, out_shape=pltpu.VMEM((1, 2, N, N), F32), in_specs=...  36 us
    unnamed x1, local copies, waits for them, and re-layouts  1.32 us

profile of v3, /device:TPU:0, one launch (start us, length us, event | category | flops | bytes accessed | tf_op | source)
XLA Modules:
  0.0 37.4 jit_solution(9450059724824717028)
XLA Ops:
  0.0 36.0 %heom.1 = f32[1,2,512,512]{3,2,1,0:T(8,128)S(1)} custom-call(s32[7]{0:T(128)} %slot_hbm.1, s32[7]{0:T(128)} %flip_hbm.1, f32[7]{0:T(128)} %rate_hbm.1, f32[7]{0:T(128)} %lower_hbm.1, s32[7,2,8,8]{3,2,1,0:T(8,128)} %mask_hbm.1, f32[1,2,512,512]{3,2,1,0:T(8,128)} %dens_hbm.1, bf16[2,512,512]{2,1,0:T(8,128)(2,1)} %ham_hbm.1, bf16[7,2,512,512]{3,2,1,0:T(8,128)(2,1)} %left_hbm.1, ...), custom_call_target="tpu_custom_call" | custom-call | tf_op jit(solution)/shard_map/heom/pallas_call | solution.py:273
  36.1 1.3 %copy.11 = f32[1,2,512,512]{3,2,1,0:T(8,128)} copy(f32[1,2,512,512]{3,2,1,0:T(8,128)S(1)} %heom.1) | data formatting | bytes 4194304

commit v4 on v3

--- a/solution.py
+++ b/solution.py
@@ -19,7 +19,7 @@
 FAR = ((8, 1), (0, 6), (6, 0))
 OTHER = (1, 0)
 LAST = NS - 1
-LATE = NS - 2
+LATE = (NS - 3, NS - 2)
 ORDER = (0, LAST) + tuple(range(1, LAST))
 RINGS = range(3)
 
@@ -42,8 +42,8 @@
     out += group(near, 0) + forward(3)
     out += group(near, 1) + steps(far[:1], 0) + forward(4)
     out += group(far[1:], 0) + forward(5)
-    out += group(near, 2) + steps(far[:1], 1) + forward(6)
-    out += group(far[1:], 1) + [("late", 1, LATE)] + forward(7) + [("relay", 1, LAST)]
+    out += group(near, 2) + [("late", 1, LATE[0])] + steps(far[:1], 1) + forward(6)
+    out += group(far[1:], 1) + [("late", 1, LATE[1])] + forward(7) + [("relay", 1, LAST)]
     out += group(near, 3) + group(far, 2) + group(far, 3)
     return out
 
@@ -140,7 +140,7 @@
     def forward(s):
         for r in RINGS:
             send(r, s, NEAR[r], OWN).wait_recv()
-            if s == LATE:
+            if s in LATE:
                 @pl.when(core == 0)
                 def _():
                     send(3 + r, s, FAR[r], r).start()

time: 37.5 us -> 38.3 us (1.021)
  Pallas kernels: 36 us -> 36.6 us
    pallas_call x1, Pallas kernels: 36 us -> 36.6 us  [body(): pl.pallas_call(kernel, out_shape=pltpu.VMEM((1, 2, N, N), F32), in_specs=...]
where the time goes in v4:
time: 38.3 us; the launch traced here: 38 us
  Pallas kernels  36.6 us (96%)
  local copies, waits for them, and re-layouts  1.32 us (3%)
    pallas_call x1, Pallas kernels, body(): pl.pallas_call(kernel, out_shape=pltpu.VMEM((1, 2, N, N), F32), in_specs=...  36.6 us
    unnamed x1, local copies, waits for them, and re-layouts  1.32 us

profile of v4, /device:TPU:0, one launch (start us, length us, event | category | flops | bytes accessed | tf_op | source)
XLA Modules:
  0.0 38.0 jit_solution(14145873458427503147)
XLA Ops:
  0.0 36.6 %heom.1 = f32[1,2,512,512]{3,2,1,0:T(8,128)S(1)} custom-call(s32[7]{0:T(128)} %slot_hbm.1, s32[7]{0:T(128)} %flip_hbm.1, f32[7]{0:T(128)} %rate_hbm.1, f32[7]{0:T(128)} %lower_hbm.1, s32[7,2,8,8]{3,2,1,0:T(8,128)} %mask_hbm.1, f32[1,2,512,512]{3,2,1,0:T(8,128)} %dens_hbm.1, bf16[2,512,512]{2,1,0:T(8,128)(2,1)} %ham_hbm.1, bf16[7,2,512,512]{3,2,1,0:T(8,128)(2,1)} %left_hbm.1, ...), custom_call_target="tpu_custom_call" | custom-call | tf_op jit(solution)/shard_map/heom/pallas_call | solution.py:273
  36.6 1.3 %copy.11 = f32[1,2,512,512]{3,2,1,0:T(8,128)} copy(f32[1,2,512,512]{3,2,1,0:T(8,128)S(1)} %heom.1) | data formatting | bytes 4194304
